TPU v7x, 256 devices: a whole 4x4x8 slice. The times are simulated.
256 devices in a mesh: firm: 16 (over y_lo, z), tm: 16 (over x, y_hi, core).
Axes of the slice: x: 4, y: 4 (y_hi: 2, y_lo: 2; y = y_hi * 2 + y_lo), z: 8, core: 2. Of those that a mesh axis runs over, the one named last changes fastest.
Arguments:
- features: bfloat16 [8192, 32, 128], P('firm', 'tm'), may hold values from -6 to 6
- cotangent: bfloat16 [8192, 32, 128], P('firm', 'tm'), may hold values from -6 to 6
- tiles: bfloat16 [64, 64, 128, 128], P('firm'), may hold values from -0.125 to 0.125
- mask: int32 [64, 64], P('firm'), may hold values 0 or 1
- w_prev: bfloat16 [2, 128, 256], replicated, may hold values from -0.375 to 0.375
- w_cur: bfloat16 [2, 128, 256], replicated, may hold values from -0.375 to 0.375
- w_self: bfloat16 [2, 128, 128], replicated, may hold values from -0.5 to 0.5
- w_nbr: bfloat16 [2, 128, 128], replicated, may hold values from -0.5 to 0.5
- dilations: int32 [2], replicated, may hold values from 1 to 2, as said below
Outputs:
- grad_features: float32 [8192, 32, 128], P('firm', 'tm')
- grad_prev: float32 [2, 128, 256], replicated
- grad_cur: float32 [2, 128, 256], replicated
- grad_self: float32 [2, 128, 128], replicated
- grad_nbr: float32 [2, 128, 128], replicated
Inputs may be any that keep to these rules, and one draw needn't show every extreme that they name: `dilations`: each layer's dilation lies between 1 and 2; some layer has dilation 1 and some layer has dilation 2.
All inputs are finite; a program needn't handle non-finite values. No bound on the sum of `mask` on one device may be relied on, other than what follows from the above.
Results may differ from a plain program's by a relative error of at most 0.007.
Values may be sent and summed in bfloat16 or wider, within the bound.
No kernel may reach another device: no remote copies, remote signals or barrier semaphores. Data moves between devices by JAX's collectives and lax.ppermute only.
A program may use at most 128 MiB of HBM per device.

v0:
```python
import jax
import jax.numpy as jnp
from jax import lax
from jax.sharding import PartitionSpec as P

L = 2


def shifted(array, axis, by):
    peers = lax.axis_size(axis)
    pairs = [(i, i + by) for i in range(peers) if 0 <= i + by < peers]
    return lax.ppermute(array, axis, pairs)


def earlier_time_days(hidden_state, dilation_factor):
    time_days = hidden_state.shape[1]
    prior = shifted(hidden_state, "tm", 1)
    paired_terms = jnp.concatenate([prior, hidden_state], axis=1)
    return lax.dynamic_slice_in_dim(paired_terms, time_days - dilation_factor, time_days, 1)


def later_time_days(reverse_flow, dilation_factor):
    time_days = reverse_flow.shape[1]
    following = shifted(reverse_flow, "tm", -1)
    paired_terms = jnp.concatenate([reverse_flow, following], axis=1)
    return lax.dynamic_slice_in_dim(paired_terms, dilation_factor, time_days, 1)


def folder(matrix, piece):
    return jnp.dot(matrix, piece, preferred_element_type=jnp.float32)


def per_device(features, cotangent, tiles, mask, w_prev, w_cur, w_self, w_nbr, dilations):
    rows, time_days, width = features.shape
    blocks_local, blocks_all, block_size, _ = tiles.shape
    all_firms = blocks_all * block_size
    masked = tiles * mask.astype(tiles.dtype)[:, :, None, None]
    row_matrix = masked.transpose(0, 2, 1, 3).reshape(rows, all_firms)
    saved = []
    hidden_state = features
    for layer_index in range(L):
        dilation_factor = dilations[layer_index]
        previous_state = earlier_time_days(hidden_state, dilation_factor)
        pre = jnp.dot(
            previous_state.reshape(-1, width),
            w_prev[layer_index],
            preferred_element_type=jnp.float32,
        )
        pre = pre + jnp.dot(
            hidden_state.reshape(-1, width), w_cur[layer_index], preferred_element_type=jnp.float32
        )
        filt = pre[:, :width]
        gate = pre[:, width:]
        gated = (jnp.tanh(filt) * jax.nn.sigmoid(gate)).astype(jnp.bfloat16)
        diffused = folder(
            row_matrix,
            lax.all_gather(gated.reshape(rows, time_days * width), "firm", axis=0, tiled=True),
        ).astype(jnp.bfloat16)
        mixed = jnp.dot(gated, w_self[layer_index], preferred_element_type=jnp.float32)
        mixed = mixed + jnp.dot(
            diffused.reshape(-1, width), w_nbr[layer_index], preferred_element_type=jnp.float32
        )
        saved.append((hidden_state, previous_state, filt, gate, gated, diffused))
        hidden_state = (
            hidden_state.astype(jnp.float32) + mixed.reshape(rows, time_days, width)
        ).astype(jnp.bfloat16)
    gradient_value = cotangent.astype(jnp.float32)
    outs_prev, outs_cur, outs_self, outs_nbr = ([], [], [], [])
    for layer_index in reversed(range(L)):
        hidden_state, previous_state, filt, gate, gated, diffused = saved[layer_index]
        dilation_factor = dilations[layer_index]
        gzb = gradient_value.astype(jnp.bfloat16).reshape(-1, width)
        outs_self.append(jnp.dot(gated.T, gzb, preferred_element_type=jnp.float32))
        outs_nbr.append(
            jnp.dot(diffused.reshape(-1, width).T, gzb, preferred_element_type=jnp.float32)
        )
        gdiff = jnp.dot(gzb, w_nbr[layer_index].T, preferred_element_type=jnp.float32).astype(
            jnp.bfloat16
        )
        gdiff_rows = gdiff.reshape(rows, time_days * width)
        spread = lax.psum_scatter(
            lax.dot_general(
                row_matrix, gdiff_rows, (((0,), (0,)), ((), ())), preferred_element_type=jnp.float32
            ),
            "firm",
            scatter_dimension=0,
            tiled=True,
        )
        ggated = jnp.dot(
            gzb, w_self[layer_index].T, preferred_element_type=jnp.float32
        ) + spread.reshape(-1, width)
        tanh_filt = jnp.tanh(filt)
        sig_gate = jax.nn.sigmoid(gate)
        gpre = jnp.concatenate(
            [
                ggated * sig_gate * (1.0 - tanh_filt * tanh_filt),
                ggated * tanh_filt * sig_gate * (1.0 - sig_gate),
            ],
            axis=1,
        ).astype(jnp.bfloat16)
        outs_cur.append(
            jnp.dot(hidden_state.reshape(-1, width).T, gpre, preferred_element_type=jnp.float32)
        )
        outs_prev.append(
            jnp.dot(previous_state.reshape(-1, width).T, gpre, preferred_element_type=jnp.float32)
        )
        reverse_flow = jnp.dot(
            gpre, w_prev[layer_index].T, preferred_element_type=jnp.float32
        ).reshape(rows, time_days, width)
        direct_path = jnp.dot(
            gpre, w_cur[layer_index].T, preferred_element_type=jnp.float32
        ).reshape(rows, time_days, width)
        gradient_value = (
            gradient_value + direct_path + later_time_days(reverse_flow, dilation_factor)
        )
    sums = lax.psum(
        (
            jnp.stack(outs_prev[::-1]),
            jnp.stack(outs_cur[::-1]),
            jnp.stack(outs_self[::-1]),
            jnp.stack(outs_nbr[::-1]),
        ),
        ("firm", "tm"),
    )
    factor = 1.0 / jnp.sqrt(jnp.float32(all_firms * time_days * lax.axis_size("tm")))
    return (gradient_value, sums[0] * factor, sums[1] * factor, sums[2] * factor, sums[3] * factor)


def solution(mesh):
    in_specs = (
        P("firm", "tm", None),
        P("firm", "tm", None),
        P("firm", None, None, None),
        P("firm", None),
        P(),
        P(),
        P(),
        P(),
        P(),
    )
    out_specs = (P("firm", "tm", None), P(), P(), P(), P())
    return jax.shard_map(
        per_device, mesh=mesh, in_specs=in_specs, out_specs=out_specs, check_vma=False
    )
```

profile of v0, /device:TPU:97, one launch (start us, length us, event | category | flops | bytes accessed | tf_op | source)
XLA Modules:
  0.0 658.3 jit_solution(12701526937728373321)
XLA Ops:
  7.2 5.4 collective-permute-start
  12.6 1.3 fusion.67
  15.2 1.2 fusion.39
  16.4 1.9 fusion.29
  18.4 1.2 convolution_add_fusion.1
  21.3 7.2 %multiply_bitcast_fusion = bf16[4,128,64,128]{3,1,2,0:T(8,128)(2,1)} fusion(bf16[4,64,128,128]{3,2,1,0:T(8,128)(2,1)} %param.11, bf16[4,64]{1,0:T(4,128)(2,1)S(1)} %convert_element_type.41), kind=kLoop, calls=%fused_computation.8 | loop fusion | flops 4194304 | bytes 16777728 | tf_op jit(solution)/shard_map/transpose | solution.py:38
  28.6 12.1 %copy.22 = bf16[4,128,64,128]{3,2,1,0:T(8,128)(2,1)} copy(bf16[4,128,64,128]{3,1,2,0:T(8,128)(2,1)} %multiply_bitcast_fusion) | data formatting | bytes 16777216 | tf_op jit(solution)/shard_map/transpose | solution.py:38
  41.0 24.6 %fusion.6 = f32[8192,256]{1,0:T(8,128)} fusion(bf16[512,256]{1,0:T(8,128)(2,1)S(1)} %reshape.86, bf16[64,8,64,128]{3,2,1,0:T(8,128)(2,1)} %bitcast.124), kind=kOutput, calls=%fused_computation.6 | convolution fusion | flops 2147483648 | bytes 17039360 | tf_op jit(solution)/shard_map/dot_general | solution.py:82
  66.7 19.3 %all-gather.3.cloned.1.call-done = bf16[8192,256]{1,0:T(8,128)(2,1)} async-done(((bf16[512,256]{1,0:T(8,128)(2,1)}), bf16[8192,256]{1,0:T(8,128)(2,1)}) %all-gather.3.cloned.1.call-update) | async-done | bytes 4194320 | tf_op jit(solution)/shard_map/all_gather | solution.py:57
  86.1 9.3 %fusion.13 = bf16[512,256]{1,0:T(8,128)(2,1)S(1)} fusion(bf16[8192,256]{1,0:T(8,128)(2,1)} %all-gather.3.cloned.1.call-done, bf16[64,8,64,128]{3,2,1,0:T(8,128)(2,1)} %bitcast.125), kind=kOutput, calls=%fused_computation.23 | convolution fusion | flops 2147614720 | bytes 12845056 | tf_op jit(solution)/shard_map/dot_general | solution.py:30
  95.9 14.7 %collective-permute-start.1 = (bf16[512,2,128]{2,1,0:T(2,128)(2,1)S(1)}, bf16[512,2,128]{2,1,0:T(2,128)(2,1)S(1)}, u32[]{:S(2)}, u32[]{:S(2)}) collective-permute-start(bf16[512,2,128]{2,1,0:T(2,128)(2,1)S(1)} %add_convert_fusion), channel_id=1, source_target_pairs={{0,1},{1,2},{2,3},{3,4},{4,5},{5,6},{6,7},{7,8},{8,9},{9,10},{10,1... | collective-permute-start | bytes 786440 | tf_op jit(solution)/shard_map/ppermute | solution.py:12
  112.3 1.7 collective-permute-done.1
  116.0 82.7 %reduce-scatter.3.cloned.1.call-done = f32[512,256]{1,0:T(8,128)} async-done(((f32[8192,256]{1,0:T(8,128)}), f32[512,256]{1,0:T(8,128)}) %reduce-scatter.3.cloned.1.call-update) | async-done | bytes 524304 | tf_op jit(solution)/shard_map/reduce_scatter | solution.py:81
  198.7 1.9 reshape.87
  200.6 2.4 multiply_convert_fusion.3
  202.9 1.8 reshape.98
  207.1 2.8 collective-permute-start.2
  211.9 7.5 %collective-permute-done.2 = f32[512,2,128]{2,0,1:T(8,128)} collective-permute-done((f32[512,2,128]{2,0,1:T(8,128)S(1)}, f32[512,2,128]{2,0,1:T(8,128)}, u32[]{:S(2)}, u32[]{:S(2)}) %collective-permute-start.2) | collective-permute-done | bytes 524320 | tf_op jit(solution)/shard_map/ppermute | solution.py:12
  219.3 2.2 fusion.68
  222.9 24.2 %fusion.2 = f32[8192,256]{1,0:T(8,128)} fusion(bf16[512,256]{1,0:T(8,128)(2,1)S(1)} %reshape.96, bf16[64,8,64,128]{3,2,1,0:T(8,128)(2,1)} %bitcast.126), kind=kOutput, calls=%fused_computation.2 | convolution fusion | flops 2147483648 | bytes 17039360 | tf_op jit(solution)/shard_map/dot_general | solution.py:82
  248.3 1.9 convolution_bitcast_fusion
  250.2 1.9 convolution_bitcast_fusion.2
  253.3 16.1 %all-gather.5.cloned.1.call-done = bf16[8192,256]{1,0:T(8,128)(2,1)} async-done(((bf16[512,256]{1,0:T(8,128)(2,1)}), bf16[8192,256]{1,0:T(8,128)(2,1)}) %all-gather.5.cloned.1.call-update) | async-done | bytes 4194320 | tf_op jit(solution)/shard_map/all_gather | solution.py:57
  269.4 9.3 %fusion.16 = bf16[512,256]{1,0:T(8,128)(2,1)S(1)} fusion(bf16[8192,256]{1,0:T(8,128)(2,1)} %all-gather.5.cloned.1.call-done, bf16[64,8,64,128]{3,2,1,0:T(8,128)(2,1)} %bitcast.127), kind=kOutput, calls=%fused_computation.24 | convolution fusion | flops 2147614720 | bytes 12845056 | tf_op jit(solution)/shard_map/dot_general | solution.py:30
  279.7 101.9 %reduce-scatter.5.cloned.1.call-done = f32[512,256]{1,0:T(8,128)} async-done(((f32[8192,256]{1,0:T(8,128)}), f32[512,256]{1,0:T(8,128)}) %reduce-scatter.5.cloned.1.call-update) | async-done | bytes 524304 | tf_op jit(solution)/shard_map/reduce_scatter | solution.py:81
  382.7 1.2 multiply_convert_fusion.1
  384.5 1.6 pad_maximum_fusion.7
  387.2 2.7 collective-permute-start.3
  391.8 254.4 %all-reduce.3.cloned.1.call-done = (f32[2,128,256]{2,1,0:T(8,128)}, f32[2,128,256]{2,1,0:T(8,128)}, f32[2,128,128]{2,1,0:T(8,128)}, f32[2,128,128]{2,1,0:T(8,128)}) async-done(((f32[2,128,256]{2,1,0:T(8,128)}, f32[2,128,256]{2,1,0:T(8,128)}, f32[2,128,128]{2,1,0:T(8,128)}, f32[2,128,128]{2,1,0:T(8,128)}), (f32[2,128,256]{2,1,0:T(8,128)}, f32[2,128,256]{2,1,0:T(8,128)}, f32[2,128,128]{2,1,0:T(8,128)}, ...) | async-done | bytes 786448 | tf_op jit(solution)/shard_map/psum | solution.py:116
  646.3 1.7 broadcast_multiply_fusion.2
  647.9 1.9 broadcast_multiply_fusion
  650.1 1.2 copy.29
  (75 shorter events, 16.2 us)
Async XLA Ops:
  7.2 78.9 %all-gather.3.cloned.1.call-start = ((), (), s32[]{:S(2)}) async-start(), calls=%async_computation.3 | async-start | bytes 4456448 | tf_op jit(solution)/shard_map/all_gather | solution.py:57
  7.2 9.2 %collective-permute-start = (bf16[512,2,128]{2,1,0:T(2,128)(2,1)}, bf16[512,2,128]{2,1,0:T(2,128)(2,1)S(1)}, u32[]{:S(2)}, u32[]{:S(2)}) collective-permute-start(bf16[512,2,128]{2,1,0:T(2,128)(2,1)} %param.9), channel_id=1, source_target_pairs={{0,1},{1,2},{2,3},{3,4},{4,5},{5,6},{6,7},{7,8},{8,9},{9,10},{10,1... | collective-permute-start | bytes 786440 | tf_op jit(solution)/shard_map/ppermute | solution.py:12
  18.4 1.2 copy-start.3
  20.6 178.1 %reduce-scatter.3.cloned.1.call-start = ((), (), s32[]{:S(2)}) async-start(), calls=%async_computation.2 | async-start | bytes 8912896 | tf_op jit(solution)/shard_map/reduce_scatter | solution.py:81
  28.6 12.1 %copy-start = (bf16[512,2,128]{2,1,0:T(2,128)(2,1)S(1)}, bf16[512,2,128]{2,1,0:T(2,128)(2,1)}, u32[]{:S(2)}) copy-start(bf16[512,2,128]{2,1,0:T(2,128)(2,1)} %param.10) | copy-start | bytes 786436
  28.6 12.1 %copy-start.12 = (bf16[2,128,128]{2,1,0:T(8,128)(2,1)S(1)}, bf16[2,128,128]{2,1,0:T(8,128)(2,1)}, u32[]{:S(2)}) copy-start(bf16[2,128,128]{2,1,0:T(8,128)(2,1)} %param.16) | copy-start | bytes 196612
  65.6 0.8 copy-start.14
  65.7 203.7 %all-gather.5.cloned.1.call-start = ((), (), s32[]{:S(2)}) async-start(), calls=%async_computation.5 | async-start | bytes 4456448 | tf_op jit(solution)/shard_map/all_gather | solution.py:57
  66.7 29.0 %copy-start.1 = (bf16[512,2,128]{2,1,0:T(2,128)(2,1)S(1)}, bf16[512,2,128]{2,1,0:T(2,128)(2,1)}, u32[]{:S(2)}) copy-start(bf16[512,2,128]{2,1,0:T(2,128)(2,1)} %param.9) | copy-start | bytes 786436
  66.7 45.3 %copy-start.9 = (bf16[2,128,256]{2,1,0:T(8,128)(2,1)S(1)}, bf16[2,128,256]{2,1,0:T(8,128)(2,1)}, u32[]{:S(2)}) copy-start(bf16[2,128,256]{2,1,0:T(8,128)(2,1)} %param.14) | copy-start | bytes 393220
  66.7 49.0 %copy-start.8 = (bf16[2,128,256]{2,1,0:T(8,128)(2,1)S(1)}, bf16[2,128,256]{2,1,0:T(8,128)(2,1)}, u32[]{:S(2)}) copy-start(bf16[2,128,256]{2,1,0:T(8,128)(2,1)} %param.13) | copy-start | bytes 393220
  95.9 18.0 %collective-permute-start.1 = (bf16[512,2,128]{2,1,0:T(2,128)(2,1)S(1)}, bf16[512,2,128]{2,1,0:T(2,128)(2,1)S(1)}, u32[]{:S(2)}, u32[]{:S(2)}) collective-permute-start(bf16[512,2,128]{2,1,0:T(2,128)(2,1)S(1)} %add_convert_fusion), channel_id=1, source_target_pairs={{0,1},{1,2},{2,3},{3,4},{4,5},{5,6},{6,7},{7,8},{8,9},{9,10},{10,1... | collective-permute-start | bytes 786440 | tf_op jit(solution)/shard_map/ppermute | solution.py:12
  115.0 0.7 copy-start.5
  204.7 176.9 %reduce-scatter.5.cloned.1.call-start = ((), (), s32[]{:S(2)}) async-start(), calls=%async_computation.4 | async-start | bytes 8912896 | tf_op jit(solution)/shard_map/reduce_scatter | solution.py:81
  207.1 12.2 %collective-permute-start.2 = (f32[512,2,128]{2,0,1:T(8,128)S(1)}, f32[512,2,128]{2,0,1:T(8,128)}, u32[]{:S(2)}, u32[]{:S(2)}) collective-permute-start(f32[512,2,128]{2,0,1:T(8,128)S(1)} %fusion.33), channel_id=1, source_target_pairs={{1,0},{2,1},{3,2},{4,3},{5,4},{6,5},{7,6},{8,7},{9,8},{10,9},{11,1... | collective-permute-start | bytes 1572872 | tf_op jit(solution)/shard_map/ppermute | solution.py:12
  247.1 1.0 copy-start.7
  247.1 1.2 copy-start.11
  247.1 3.1 copy-start.6
  247.1 399.1 %all-reduce.3.cloned.1.call-start = ((), (), s32[]{:S(2)}) async-start(), calls=%async_computation.6 | async-start | bytes 1572864 | tf_op jit(solution)/shard_map/psum | solution.py:116
  253.3 130.9 %copy-start.4 = (bf16[512,2,128]{2,1,0:T(2,128)(2,1)S(1)}, bf16[512,2,128]{2,1,0:T(2,128)(2,1)}, u32[]{:S(2)}) copy-start(bf16[512,2,128]{2,1,0:T(2,128)(2,1)} %copy-done.3) | copy-start | bytes 786436
  278.7 371.1 %copy-start.2 = (f32[512,2,128]{2,0,1:T(8,128)S(1)}, f32[512,2,128]{2,0,1:T(8,128)}, u32[]{:S(2)}) copy-start(f32[512,2,128]{2,0,1:T(8,128)} %get-tuple-element.27) | copy-start | bytes 1572868
  278.7 371.1 %copy-start.10 = (bf16[2,128,256]{2,1,0:T(8,128)(2,1)S(1)}, bf16[2,128,256]{2,1,0:T(8,128)(2,1)}, u32[]{:S(2)}) copy-start(bf16[2,128,256]{2,1,0:T(8,128)(2,1)} %param.14) | copy-start | bytes 393220
  279.7 106.4 %copy-start.13 = (f32[1,128,256]{2,1,0:T(8,128)S(1)}, f32[1,128,256]{2,1,0:T(8,128)}, u32[]{:S(2)}) copy-start(f32[1,128,256]{2,1,0:T(8,128)} %convolution_bitcast_fusion.2) | copy-start | bytes 393220
  387.2 262.6 %collective-permute-start.3 = (f32[512,2,128]{2,0,1:T(8,128)S(1)}, f32[512,2,128]{2,0,1:T(8,128)S(1)}, u32[]{:S(2)}, u32[]{:S(2)}) collective-permute-start(f32[512,2,128]{2,0,1:T(8,128)S(1)} %fusion.30), channel_id=1, source_target_pairs={{1,0},{2,1},{3,2},{4,3},{5,4},{6,5},{7,6},{8,7},{9,8},{10,9},{11,1... | collective-permute-start | bytes 1572872 | tf_op jit(solution)/shard_map/ppermute | solution.py:12
Sparse Core Ops, SparseCore 0:
  20.7 65.2 all-gather.2
  88.6 110.0 reduce-scatter.2
  204.8 64.4 all-gather.4
  271.8 109.7 reduce-scatter.4
  387.9 258.2 all-reduce.2
where the time goes:
time: 669 us; the launch traced here: 658 us
  waiting for transfers between devices  484 us (72%)
  matrix products  83.9 us (13%)
  starting transfers between devices  26.1 us (4%)
  local copies, waits for them, and re-layouts  25.1 us (4%)
  between operations  21 us (3%)
  other arithmetic  18.5 us (3%)
    psum x1, waiting for transfers between devices, per_device(): lax.psum((jnp.stack(outs_prev[::-1]), jnp.stack(outs_cur[::-1]), jnp.stac...  254 us
    reduce_scatter x2, waiting for transfers between devices, per_device(): lax.psum_scatter(lax.dot_general(row_matrix, gdiff_rows, (((0,), (0,)), (...  185 us
    dot_general x2, matrix products, per_device(): lax.dot_general(row_matrix, gdiff_rows, (((0,), (0,)), ((), ())), preferr...  48.8 us
    all_gather x2, waiting for transfers between devices, per_device(): lax.all_gather(gated.reshape(rows, time_days * width), 'firm', axis=0, ti...  35.4 us
    ppermute x4, starting transfers between devices, shifted(): return lax.ppermute(array, axis, pairs)  25.6 us
    dot_general x2, matrix products, folder(): return jnp.dot(matrix, piece, preferred_element_type=jnp.float32)  18.6 us
  transfers between devices with their start and end apart: 9, of which 7 were waited for; matrix products, arithmetic and copies ran while one was open for 16% of the time, Pallas kernels for 0%

commit v1 on v0

--- a/solution.py
+++ b/solution.py
@@ -4,6 +4,11 @@
 from jax.sharding import PartitionSpec as P
 
 L = 2
+
+
+def swapped_in(array, mesh_axis, dim):
+    sent = jnp.stack([array] * lax.axis_size(mesh_axis))
+    return jnp.concatenate(lax.all_to_all(sent, mesh_axis, 0, 0), axis=dim)
 
 
 def shifted(array, axis, by):
@@ -53,8 +58,7 @@
         gate = pre[:, width:]
         gated = (jnp.tanh(filt) * jax.nn.sigmoid(gate)).astype(jnp.bfloat16)
         diffused = folder(
-            row_matrix,
-            lax.all_gather(gated.reshape(rows, time_days * width), "firm", axis=0, tiled=True),
+            row_matrix, swapped_in(gated.reshape(rows, time_days * width), "firm", 0)
         ).astype(jnp.bfloat16)
         mixed = jnp.dot(gated, w_self[layer_index], preferred_element_type=jnp.float32)
         mixed = mixed + jnp.dot(

time: 669 us -> 763 us (1.14)
  waiting for transfers between devices: 484 us -> 572 us
  starting transfers between devices: 26.1 us -> 34.3 us
    all_to_all x0 -> x2, waiting for transfers between devices: none -> 243 us  [swapped_in(): return jnp.concatenate(lax.all_to_all(sent, mesh_axis, 0, 0), axis=dim)]
    reduce_scatter x2, waiting for transfers between devices: 185 us -> 58.7 us  [per_device(): lax.psum_scatter(lax.dot_general(row_matrix, gdiff_rows, (((0,), (0,)), (...]
    all_gather x2 -> x0, waiting for transfers between devices: 35.4 us -> none  [per_device(): lax.all_gather(gated.reshape(rows, time_days * width), 'firm', axis=0, ti...]
    all_to_all x0 -> x2, starting transfers between devices: none -> 16.1 us  [swapped_in(): return jnp.concatenate(lax.all_to_all(sent, mesh_axis, 0, 0), axis=dim)]
    ppermute x4, starting transfers between devices: 25.6 us -> 17.9 us  [shifted(): return lax.ppermute(array, axis, pairs)]
  transfers between devices with their start and end apart: 9 -> 9, of which waited for: 7 -> 8; matrix products, arithmetic and copies ran while one was open for 16% -> 5% of each run, Pallas kernels for 0% -> 0%
where the time goes in v1:
time: 763 us; the launch traced here: 754 us
  waiting for transfers between devices  572 us (75%)
  matrix products  83.2 us (11%)
  starting transfers between devices  34.3 us (4%)
  local copies, waits for them, and re-layouts  25.1 us (3%)
  between operations  21 us (3%)
  other arithmetic  17.5 us (2%)
    psum x1, waiting for transfers between devices, per_device(): lax.psum((jnp.stack(outs_prev[::-1]), jnp.stack(outs_cur[::-1]), jnp.stac...  261 us
    all_to_all x2, waiting for transfers between devices, swapped_in(): return jnp.concatenate(lax.all_to_all(sent, mesh_axis, 0, 0), axis=dim)  243 us
    reduce_scatter x2, waiting for transfers between devices, per_device(): lax.psum_scatter(lax.dot_general(row_matrix, gdiff_rows, (((0,), (0,)), (...  58.7 us
    dot_general x2, matrix products, per_device(): lax.dot_general(row_matrix, gdiff_rows, (((0,), (0,)), ((), ())), preferr...  48.7 us
    dot_general x2, matrix products, folder(): return jnp.dot(matrix, piece, preferred_element_type=jnp.float32)  18.9 us
    ppermute x4, starting transfers between devices, shifted(): return lax.ppermute(array, axis, pairs)  17.9 us
    all_to_all x2, starting transfers between devices, swapped_in(): return jnp.concatenate(lax.all_to_all(sent, mesh_axis, 0, 0), axis=dim)  16.1 us
  transfers between devices with their start and end apart: 9, of which 8 were waited for; matrix products, arithmetic and copies ran while one was open for 5% of the time, Pallas kernels for 0%

profile of v1, /device:TPU:97, one launch (start us, length us, event | category | flops | bytes accessed | tf_op | source)
XLA Modules:
  0.0 753.7 jit_solution(4745843494310478073)
XLA Ops:
  7.9 7.2 multiply_bitcast_fusion
  15.1 12.1 %copy.22 = bf16[4,128,64,128]{3,2,1,0:T(8,128)(2,1)} copy(bf16[4,128,64,128]{3,1,2,0:T(8,128)(2,1)} %multiply_bitcast_fusion) | data formatting | bytes 16777216 | tf_op jit(solution)/shard_map/transpose | solution.py:43
  27.6 24.5 %fusion.6 = f32[8192,256]{1,0:T(8,128)} fusion(bf16[512,256]{1,0:T(8,128)(2,1)S(1)} %reshape.90, bf16[64,8,64,128]{3,2,1,0:T(8,128)(2,1)} %bitcast.126), kind=kOutput, calls=%fused_computation.6 | convolution fusion | flops 2147483648 | bytes 17039360 | tf_op jit(solution)/shard_map/dot_general | solution.py:86
  53.1 5.4 collective-permute-start
  60.6 1.1 collective-permute-done
  64.0 2.4 stack.42
  66.5 7.2 all-to-all-start
  74.0 127.2 %all-to-all-done = bf16[16,512,256]{2,1,0:T(8,128)(2,1)} async-done(((bf16[16,512,256]{2,1,0:T(8,128)(2,1)}), bf16[16,512,256]{2,1,0:T(8,128)(2,1)}, u32[]{:S(2)}, u32[]{:S(2)}) %all-to-all-start) | async-done | bytes 4194336 | tf_op jit(solution)/shard_map/all_to_all | solution.py:11
  201.2 9.4 %fusion.13 = bf16[512,256]{1,0:T(8,128)(2,1)S(1)} fusion(bf16[8192,256]{1,0:T(8,128)(2,1)} %bitcast.10, bf16[64,8,64,128]{3,2,1,0:T(8,128)(2,1)} %bitcast.127), kind=kOutput, calls=%fused_computation.23 | convolution fusion | flops 2147614720 | bytes 12845056 | tf_op jit(solution)/shard_map/dot_general | solution.py:35
  211.2 7.4 collective-permute-start.1
  220.2 1.7 collective-permute-done.1
  222.9 1.3 convolution_add_fusion
  224.1 19.6 %reduce-scatter.3.cloned.1.call-done = f32[512,256]{1,0:T(8,128)} async-done(((f32[8192,256]{1,0:T(8,128)}), f32[512,256]{1,0:T(8,128)}) %reduce-scatter.3.cloned.1.call-update) | async-done | bytes 524304 | tf_op jit(solution)/shard_map/reduce_scatter | solution.py:85
  244.8 2.4 multiply_convert_fusion.3
  248.2 2.8 collective-permute-start.2
  253.0 7.5 collective-permute-done.2
  260.4 2.2 fusion.68
  264.0 24.1 %fusion.2 = f32[8192,256]{1,0:T(8,128)} fusion(bf16[512,256]{1,0:T(8,128)(2,1)S(1)} %reshape.100, bf16[64,8,64,128]{3,2,1,0:T(8,128)(2,1)} %bitcast.128), kind=kOutput, calls=%fused_computation.2 | convolution fusion | flops 2147483648 | bytes 17039360 | tf_op jit(solution)/shard_map/dot_general | solution.py:86
  289.2 2.4 stack.53
  291.6 8.8 %all-to-all-start.1 = ((bf16[16,512,256]{2,1,0:T(8,128)(2,1)}), bf16[16,512,256]{2,1,0:T(8,128)(2,1)}, u32[]{:S(2)}, u32[]{:S(2)}) async-start(bf16[16,512,256]{2,1,0:T(8,128)(2,1)} %stack.53), calls=%async_computation.3 | async-start | bytes 8388608 | tf_op jit(solution)/shard_map/all_to_all | solution.py:11
  301.0 1.9 convolution_bitcast_fusion
  302.9 1.9 convolution_bitcast_fusion.2
  306.0 115.5 %all-to-all-done.1 = bf16[16,512,256]{2,1,0:T(8,128)(2,1)} async-done(((bf16[16,512,256]{2,1,0:T(8,128)(2,1)}), bf16[16,512,256]{2,1,0:T(8,128)(2,1)}, u32[]{:S(2)}, u32[]{:S(2)}) %all-to-all-start.1) | async-done | bytes 4194336 | tf_op jit(solution)/shard_map/all_to_all | solution.py:11
  421.5 9.5 %fusion.16 = bf16[512,256]{1,0:T(8,128)(2,1)S(1)} fusion(bf16[8192,256]{1,0:T(8,128)(2,1)} %bitcast.35, bf16[64,8,64,128]{3,2,1,0:T(8,128)(2,1)} %bitcast.129), kind=kOutput, calls=%fused_computation.24 | convolution fusion | flops 2147614720 | bytes 12845056 | tf_op jit(solution)/shard_map/dot_general | solution.py:35
  432.0 39.1 %reduce-scatter.5.cloned.1.call-done = f32[512,256]{1,0:T(8,128)} async-done(((f32[8192,256]{1,0:T(8,128)}), f32[512,256]{1,0:T(8,128)}) %reduce-scatter.5.cloned.1.call-update) | async-done | bytes 524304 | tf_op jit(solution)/shard_map/reduce_scatter | solution.py:85
  472.2 1.2 multiply_convert_fusion.1
  474.0 1.6 pad_maximum_fusion.7
  476.7 2.3 collective-permute-start.3
  480.9 260.7 %all-reduce.3.cloned.1.call-done = (f32[2,128,256]{2,1,0:T(8,128)}, f32[2,128,256]{2,1,0:T(8,128)}, f32[2,128,128]{2,1,0:T(8,128)}, f32[2,128,128]{2,1,0:T(8,128)}) async-done(((f32[2,128,256]{2,1,0:T(8,128)}, f32[2,128,256]{2,1,0:T(8,128)}, f32[2,128,128]{2,1,0:T(8,128)}, f32[2,128,128]{2,1,0:T(8,128)}), (f32[2,128,256]{2,1,0:T(8,128)}, f32[2,128,256]{2,1,0:T(8,128)}, f32[2,128,128]{2,1,0:T(8,128)}, ...) | async-done | bytes 786448 | tf_op jit(solution)/shard_map/psum | solution.py:120
  741.6 1.7 broadcast_multiply_fusion.2
  743.3 1.9 broadcast_multiply_fusion
  745.5 1.2 copy.29
  (81 shorter events, 17.4 us)
Async XLA Ops:
  7.2 236.6 %reduce-scatter.3.cloned.1.call-start = ((), (), s32[]{:S(2)}) async-start(), calls=%async_computation.4 | async-start | bytes 8912896 | tf_op jit(solution)/shard_map/reduce_scatter | solution.py:85
  15.1 12.1 %copy-start = (bf16[512,2,128]{2,1,0:T(2,128)(2,1)S(1)}, bf16[512,2,128]{2,1,0:T(2,128)(2,1)}, u32[]{:S(2)}) copy-start(bf16[512,2,128]{2,1,0:T(2,128)(2,1)} %param.10) | copy-start | bytes 786436
  15.1 12.1 %copy-start.14 = (bf16[2,128,128]{2,1,0:T(8,128)(2,1)S(1)}, bf16[2,128,128]{2,1,0:T(8,128)(2,1)}, u32[]{:S(2)}) copy-start(bf16[2,128,128]{2,1,0:T(8,128)(2,1)} %param.16) | copy-start | bytes 196612
  52.1 0.9 copy-start.1
  52.2 6.3 copy-start.17
  52.2 8.2 %copy-start.9 = (bf16[2,128,256]{2,1,0:T(8,128)(2,1)S(1)}, bf16[2,128,256]{2,1,0:T(8,128)(2,1)}, u32[]{:S(2)}) copy-start(bf16[2,128,256]{2,1,0:T(8,128)(2,1)} %param.14) | copy-start | bytes 393220
  52.2 11.3 %copy-start.8 = (bf16[2,128,256]{2,1,0:T(8,128)(2,1)S(1)}, bf16[2,128,256]{2,1,0:T(8,128)(2,1)}, u32[]{:S(2)}) copy-start(bf16[2,128,256]{2,1,0:T(8,128)(2,1)} %param.13) | copy-start | bytes 393220
  53.1 8.7 %collective-permute-start = (bf16[512,2,128]{2,1,0:T(2,128)(2,1)S(1)}, bf16[512,2,128]{2,1,0:T(2,128)(2,1)S(1)}, u32[]{:S(2)}, u32[]{:S(2)}) collective-permute-start(bf16[512,2,128]{2,1,0:T(2,128)(2,1)S(1)} %copy-done.1), channel_id=1, source_target_pairs={{0,1},{1,2},{2,3},{3,4},{4,5},{5,6},{6,7},{7,8},{8,9},{9,10},{10,1... | collective-permute-start | bytes 786440 | tf_op jit(solution)/shard_map/ppermute | solution.py:17
  62.7 0.7 copy-start.3
  63.4 10.3 %copy-start.16 = (bf16[2,128,128]{2,1,0:T(8,128)(2,1)S(1)}, bf16[2,128,128]{2,1,0:T(8,128)(2,1)}, u32[]{:S(2)}) copy-start(bf16[2,128,128]{2,1,0:T(8,128)(2,1)} %param.15) | copy-start | bytes 196612
  66.5 134.7 %all-to-all-start = ((bf16[16,512,256]{2,1,0:T(8,128)(2,1)}), bf16[16,512,256]{2,1,0:T(8,128)(2,1)}, u32[]{:S(2)}, u32[]{:S(2)}) async-start(bf16[16,512,256]{2,1,0:T(8,128)(2,1)} %stack.42), calls=%async_computation.1 | async-start | bytes 8388608 | tf_op jit(solution)/shard_map/all_to_all | solution.py:11
  73.7 397.4 %reduce-scatter.5.cloned.1.call-start = ((), (), s32[]{:S(2)}) async-start(), calls=%async_computation.5 | async-start | bytes 8912896 | tf_op jit(solution)/shard_map/reduce_scatter | solution.py:85
  211.2 10.7 %collective-permute-start.1 = (bf16[512,2,128]{2,1,0:T(2,128)(2,1)S(1)}, bf16[512,2,128]{2,1,0:T(2,128)(2,1)S(1)}, u32[]{:S(2)}, u32[]{:S(2)}) collective-permute-start(bf16[512,2,128]{2,1,0:T(2,128)(2,1)S(1)} %add_convert_fusion), channel_id=1, source_target_pairs={{0,1},{1,2},{2,3},{3,4},{4,5},{5,6},{6,7},{7,8},{8,9},{9,10},{10,1... | collective-permute-start | bytes 786440 | tf_op jit(solution)/shard_map/ppermute | solution.py:17
  222.9 24.3 %copy-start.5 = (bf16[512,2,128]{2,1,0:T(2,128)(2,1)}, bf16[512,2,128]{2,1,0:T(2,128)(2,1)S(1)}, u32[]{:S(2)}) copy-start(bf16[512,2,128]{2,1,0:T(2,128)(2,1)S(1)} %fusion.28) | copy-start | bytes 786436
  247.2 0.7 copy-start.11
  247.2 1.0 copy-start.13
  248.2 12.2 %collective-permute-start.2 = (f32[512,2,128]{2,0,1:T(8,128)S(1)}, f32[512,2,128]{2,0,1:T(8,128)}, u32[]{:S(2)}, u32[]{:S(2)}) collective-permute-start(f32[512,2,128]{2,0,1:T(8,128)S(1)} %fusion.33), channel_id=1, source_target_pairs={{1,0},{2,1},{3,2},{4,3},{5,4},{6,5},{7,6},{8,7},{9,8},{10,9},{11,1... | collective-permute-start | bytes 1572872 | tf_op jit(solution)/shard_map/ppermute | solution.py:17
  288.1 0.9 copy-start.7
  288.2 14.7 %copy-start.6 = (bf16[512,2,128]{2,1,0:T(2,128)(2,1)S(1)}, bf16[512,2,128]{2,1,0:T(2,128)(2,1)}, u32[]{:S(2)}) copy-start(bf16[512,2,128]{2,1,0:T(2,128)(2,1)} %copy-done.5) | copy-start | bytes 786436
  291.6 9.4 %copy-start.12 = (bf16[1024,128]{1,0:T(8,128)(2,1)S(1)}, bf16[1024,128]{1,0:T(8,128)(2,1)}, u32[]{:S(2)}) copy-start(bf16[1024,128]{1,0:T(8,128)(2,1)} %copy-done.11) | copy-start | bytes 786436
  291.6 129.9 %all-to-all-start.1 = ((bf16[16,512,256]{2,1,0:T(8,128)(2,1)}), bf16[16,512,256]{2,1,0:T(8,128)(2,1)}, u32[]{:S(2)}, u32[]{:S(2)}) async-start(bf16[16,512,256]{2,1,0:T(8,128)(2,1)} %stack.53), calls=%async_computation.3 | async-start | bytes 8388608 | tf_op jit(solution)/shard_map/all_to_all | solution.py:11
  300.4 441.2 %all-reduce.3.cloned.1.call-start = ((), (), s32[]{:S(2)}) async-start(), calls=%async_computation.6 | async-start | bytes 1572864 | tf_op jit(solution)/shard_map/psum | solution.py:120
  421.5 52.2 %copy-start.4 = (bf16[512,2,128]{2,1,0:T(2,128)(2,1)S(1)}, bf16[512,2,128]{2,1,0:T(2,128)(2,1)}, u32[]{:S(2)}) copy-start(bf16[512,2,128]{2,1,0:T(2,128)(2,1)} %copy-done.3) | copy-start | bytes 786436
  431.0 314.2 %copy-start.2 = (f32[512,2,128]{2,0,1:T(8,128)S(1)}, f32[512,2,128]{2,0,1:T(8,128)}, u32[]{:S(2)}) copy-start(f32[512,2,128]{2,0,1:T(8,128)} %get-tuple-element.27) | copy-start | bytes 1572868
  431.0 314.2 %copy-start.10 = (bf16[2,128,256]{2,1,0:T(8,128)(2,1)S(1)}, bf16[2,128,256]{2,1,0:T(8,128)(2,1)}, u32[]{:S(2)}) copy-start(bf16[2,128,256]{2,1,0:T(8,128)(2,1)} %param.14) | copy-start | bytes 393220
  432.0 43.6 %copy-start.15 = (f32[1,128,256]{2,1,0:T(8,128)S(1)}, f32[1,128,256]{2,1,0:T(8,128)}, u32[]{:S(2)}) copy-start(f32[1,128,256]{2,1,0:T(8,128)} %convolution_bitcast_fusion.2) | copy-start | bytes 393220
  476.7 268.5 %collective-permute-start.3 = (f32[512,2,128]{2,0,1:T(8,128)S(1)}, f32[512,2,128]{2,0,1:T(8,128)S(1)}, u32[]{:S(2)}, u32[]{:S(2)}) collective-permute-start(f32[512,2,128]{2,0,1:T(8,128)S(1)} %fusion.30), channel_id=1, source_target_pairs={{1,0},{2,1},{3,2},{4,3},{5,4},{6,5},{7,6},{8,7},{9,8},{10,9},{11,1... | collective-permute-start | bytes 1572872 | tf_op jit(solution)/shard_map/ppermute | solution.py:17
Sparse Core Ops, SparseCore 0:
  52.3 191.3 reduce-scatter.2
  288.3 182.7 reduce-scatter.4
  477.6 264.0 all-reduce.2
